TPU v7x, 512 devices: a whole 4x4x16 slice. The times are simulated.
512 devices in a mesh: section: 8 (over y, core), expert: 64 (over z, x).
Axes of the slice: x: 4, y: 4, z: 16, core: 2. Of those that a mesh axis runs over, the one named last changes fastest.
Arguments:
- tokens: bfloat16 [8, 4096, 4096], P('section', 'expert'), may hold values from -6 to 6
- expert_ids: int32 [8, 1, 4096, 1], P('section'), may hold values from 0 to 7; in each aligned block of 64 rows (0 to 63, 64 to 127, ..., all dimensions but the last counted through in order) at most 12 rows name the same one
- gate_weights: float32 [8, 1, 4096, 1], P('section'), may hold values from 0.2 to 1
- norm_gain: bfloat16 [8, 4096], P('section'), may hold values from 0.099609375 to 1.8984375
- w_gate: bfloat16 [8, 4096, 8192], P('section', None, 'expert'), may hold values from -0.09375 to 0.09375
- w_up: bfloat16 [8, 4096, 8192], P('section', None, 'expert'), may hold values from -0.09375 to 0.09375
- w_down: bfloat16 [8, 8192, 4096], P('section', 'expert'), may hold values from -0.1875 to 0.1875
Outputs:
- finished: bfloat16 [8, 4096, 4096], P('section', 'expert')
Inputs may be any that keep to these rules, and one draw needn't show every extreme that they name: `expert_ids`: each row names one expert (1 = 1). In every aligned block of 64 rows (one device's rows at one section and stop) no expert is named by more than 12 rows, and some block names some expert exactly 12 times.
All inputs are finite; a program needn't handle non-finite values.
Results may differ from a plain program's by a relative error of at most 0.0041.
Values may be sent and summed in bfloat16 or wider, within the bound.
A program may use at most 64 MiB of HBM per device.

v0:
```python
import jax
import jax.numpy as jnp
from jax import lax
from jax.sharding import PartitionSpec as P

EXPS = 8
TOPK = 1
CAP = 12


def from_behind(value, axis, steps):
    count = lax.axis_size(axis)
    pairs = [(source, (source + steps) % count) for source in range(count)]
    return lax.ppermute(value, axis, pairs)


def tables(route_ids, route_weights, blocks, row_count, width, experts, slot_cap):
    hot_map = (route_ids[:, :, None] == jnp.arange(experts, dtype=jnp.int32)).astype(jnp.int32)
    hot_map = hot_map.reshape(blocks, row_count * width, experts)
    slot_rank = jnp.cumsum(hot_map, axis=1) - 1
    chosen = hot_map[..., None] * (
        slot_rank[..., None] == jnp.arange(slot_cap, dtype=jnp.int32)
    ).astype(jnp.int32)
    chosen = chosen.reshape(blocks, row_count, width, experts, slot_cap)
    placed = jnp.sum(chosen, axis=2)
    scaled = jnp.sum(
        chosen.astype(jnp.float32) * route_weights.reshape(blocks, row_count, width, 1, 1), axis=2
    )
    return (placed, scaled)


def local(tokens, expert_ids, gate_weights, norm_gain, w_gate, w_up, w_down):
    devices = lax.axis_size("expert")
    groups = devices // EXPS
    my_index = lax.axis_index("expert")
    row_count = tokens.shape[1]
    width = tokens.shape[2]
    gate_cols = w_gate[0]
    up_cols = w_up[0]
    down_rows = w_down[0]
    gain = norm_gain[0].astype(jnp.float32)
    current = tokens[0]
    wide_state = current.astype(jnp.float32)
    meansq = jnp.mean(wide_state * wide_state, axis=-1, keepdims=True)
    normed = (wide_state * lax.rsqrt(meansq + 1e-06) * gain).astype(jnp.bfloat16)
    route_ids = expert_ids[0, 0]
    route_weights = gate_weights[0, 0]
    own_ids = lax.dynamic_slice_in_dim(route_ids, my_index * row_count, row_count, 0)
    own_weights = lax.dynamic_slice_in_dim(route_weights, my_index * row_count, row_count, 0)
    placed, scaled = tables(own_ids, own_weights, 1, row_count, TOPK, EXPS, CAP)
    own_scaled = scaled[0]
    outgoing = jnp.einsum(
        "rec,rd->ecd", placed[0].astype(jnp.bfloat16), normed, preferred_element_type=jnp.float32
    ).astype(jnp.bfloat16)
    outgoing = jnp.broadcast_to(outgoing[:, None], (EXPS, groups, CAP, width)).reshape(
        devices, CAP, width
    )
    slotted = lax.all_to_all(outgoing, "expert", split_axis=0, concat_axis=0, tiled=True)
    flat_rows = slotted.reshape(-1, width)
    gate = jnp.dot(flat_rows, gate_cols, preferred_element_type=jnp.float32)
    upward = jnp.dot(flat_rows, up_cols, preferred_element_type=jnp.float32)
    hidden = (jax.nn.silu(gate) * upward).astype(jnp.bfloat16)
    partial_value = jnp.dot(hidden, down_rows, preferred_element_type=jnp.float32).astype(
        jnp.bfloat16
    )
    returned = partial_value.reshape(slotted.shape)
    returned = lax.all_to_all(returned, "expert", split_axis=0, concat_axis=0, tiled=True)
    summed = jnp.sum(returned.reshape(EXPS, groups, CAP, width).astype(jnp.float32), axis=1)
    expert_out = jnp.einsum("rec,ecd->rd", own_scaled, summed, precision=lax.Precision.HIGHEST)
    current = (wide_state + expert_out).astype(jnp.bfloat16)
    current = from_behind(current, "section", 1)
    return current[None]


def solution(mesh):
    placed = (
        P("section", "expert", None),
        P("section", None, None, None),
        P("section", None, None, None),
        P("section", None),
        P("section", None, "expert"),
        P("section", None, "expert"),
        P("section", "expert", None),
    )
    return jax.shard_map(
        local, mesh=mesh, in_specs=placed, out_specs=P("section", "expert", None), check_vma=False
    )
```

profile of v0, /device:TPU:1, one launch (start us, length us, event | category | flops | bytes accessed | tf_op | source)
XLA Modules:
  0.0 822.1 jit_solution(15696830392368456211)
XLA Ops:
  0.0 0.0 copy-start
  0.0 0.8 dynamic-slice_bitcast_fusion.1
  0.8 0.1 fusion.31
  0.9 0.1 copy.11
  1.0 0.1 reduce_window_sum.11
  1.1 1.3 fusion.3
  2.3 0.7 mul.71
  3.1 0.1 copy.10
  3.1 1.5 convolution_convert_fusion.1
  4.7 1.0 broadcast_in_dim.4
  5.7 383.5 %all_to_all.10 = bf16[64,12,4096]{2,1,0:T(8,128)(2,1)} all-to-all(bf16[64,12,4096]{2,1,0:T(8,128)(2,1)S(1)} %bitcast.40), channel_id=1, replica_groups=mesh['section'=8,'expert'=64] {'expert'}, dimensions={0} | all-to-all | bytes 12582912 | tf_op jit(solution)/shard_map/all_to_all | solution.py:58
  389.3 0.0 copy-start.3
  389.3 10.1 %reshape.113 = bf16[768,4096]{1,0:T(8,128)(2,1)} reshape(bf16[64,12,4096]{2,1,0:T(8,128)(2,1)} %all_to_all.10) | data formatting | bytes 12582912 | tf_op jit(solution)/shard_map/reshape | solution.py:59
  399.3 0.0 copy-done.3
  399.3 0.0 copy-start.2
  399.3 4.7 fusion.9
  404.0 0.0 copy-done
  404.0 0.0 copy-done.2
  404.0 12.1 %convolution_convert_fusion = bf16[768,4096]{1,0:T(8,128)(2,1)} fusion(bf16[768,4096]{1,0:T(8,128)(2,1)} %reshape.113, bf16[1,128,4096]{2,1,0:T(8,128)(2,1)S(1)} %copy-done, bf16[1,4096,128]{2,1,0:T(8,128)(2,1)S(1)} %copy-done.2, f32[768,128]{1,0:T(8,128)S(1)} %fusion.9), kind=kOutput, calls=%fused_computation.1 | convolution fusion | flops 1614348288 | bytes 15073280 | tf_op jit(solution)/shard_map/dot_general | solution.py:63
  416.1 9.8 %reshape.114 = bf16[64,12,4096]{2,1,0:T(8,128)(2,1)} reshape(bf16[768,4096]{1,0:T(8,128)(2,1)} %convolution_convert_fusion) | data formatting | bytes 12582912 | tf_op jit(solution)/shard_map/reshape | solution.py:66
  425.9 11.1 %all-to-all-start.1 = ((bf16[64,12,4096]{2,1,0:T(8,128)(2,1)}), bf16[64,12,4096]{2,1,0:T(8,128)(2,1)}, u32[]{:S(2)}, u32[]{:S(2)}) async-start(bf16[64,12,4096]{2,1,0:T(8,128)(2,1)} %reshape.114), calls=%async_computation.1 | async-start | bytes 16777216 | tf_op jit(solution)/shard_map/all_to_all | solution.py:67
  437.0 0.0 copy-start.1
  437.1 0.8 dynamic-slice_bitcast_fusion
  437.8 360.7 %all-to-all-done.1 = bf16[64,12,4096]{2,1,0:T(8,128)(2,1)} async-done(((bf16[64,12,4096]{2,1,0:T(8,128)(2,1)}), bf16[64,12,4096]{2,1,0:T(8,128)(2,1)}, u32[]{:S(2)}, u32[]{:S(2)}) %all-to-all-start.1) | async-done | bytes 6291488 | tf_op jit(solution)/shard_map/all_to_all | solution.py:67
  798.6 5.1 convert_reduce_fusion
  803.7 0.0 copy-done.1
  803.7 1.3 fusion.1
  805.0 10.2 %collective-permute-start = (bf16[64,4096]{1,0:T(8,128)(2,1)S(1)}, bf16[64,4096]{1,0:T(8,128)(2,1)S(1)}, u32[]{:S(2)}, u32[]{:S(2)}) collective-permute-start(bf16[64,4096]{1,0:T(8,128)(2,1)S(1)} %fusion.1), channel_id=1, source_target_pairs={{0,64},{64,128},{128,192},{192,256},{256,320},{320,384},{384,448},... | collective-permute-start | bytes 1572872 | tf_op jit(solution)/shard_map/ppermute | solution.py:14
  815.2 6.1 collective-permute-done
  821.3 0.8 copy.13
  (2 shorter events, 0.0 us)
Async XLA Ops:
  0.0 404.0 %copy-start = (bf16[1,128,4096]{2,1,0:T(8,128)(2,1)S(1)}, bf16[1,128,4096]{2,1,0:T(8,128)(2,1)}, u32[]{:S(2)}) copy-start(bf16[1,128,4096]{2,1,0:T(8,128)(2,1)} %param.13) | copy-start | bytes 3145732
  389.3 10.1 %copy-start.3 = (bf16[1,4096,128]{2,1,0:T(8,128)(2,1)S(1)}, bf16[1,4096,128]{2,1,0:T(8,128)(2,1)}, u32[]{:S(2)}) copy-start(bf16[1,4096,128]{2,1,0:T(8,128)(2,1)} %param.11) | copy-start | bytes 3145732
  399.3 4.7 copy-start.2
  425.9 372.7 %all-to-all-start.1 = ((bf16[64,12,4096]{2,1,0:T(8,128)(2,1)}), bf16[64,12,4096]{2,1,0:T(8,128)(2,1)}, u32[]{:S(2)}, u32[]{:S(2)}) async-start(bf16[64,12,4096]{2,1,0:T(8,128)(2,1)} %reshape.114), calls=%async_computation.1 | async-start | bytes 16777216 | tf_op jit(solution)/shard_map/all_to_all | solution.py:67
  437.0 366.7 %copy-start.1 = (bf16[1,64,4096]{2,1,0:T(8,128)(2,1)S(1)}, bf16[1,64,4096]{2,1,0:T(8,128)(2,1)}, u32[]{:S(2)}) copy-start(bf16[1,64,4096]{2,1,0:T(8,128)(2,1)} %param.7) | copy-start | bytes 1572868
  805.0 16.3 %collective-permute-start = (bf16[64,4096]{1,0:T(8,128)(2,1)S(1)}, bf16[64,4096]{1,0:T(8,128)(2,1)S(1)}, u32[]{:S(2)}, u32[]{:S(2)}) collective-permute-start(bf16[64,4096]{1,0:T(8,128)(2,1)S(1)} %fusion.1), channel_id=1, source_target_pairs={{0,64},{64,128},{128,192},{192,256},{256,320},{320,384},{384,448},... | collective-permute-start | bytes 1572872 | tf_op jit(solution)/shard_map/ppermute | solution.py:14
where the time goes:
time: 824 us; the launch traced here: 822 us
  blocking collectives  384 us (47%)
  waiting for transfers between devices  367 us (45%)
  local copies, waits for them, and re-layouts  23.4 us (3%)
  starting transfers between devices  21.3 us (3%)
  matrix products  19.5 us (2%)
    all_to_all x1, blocking collectives, local(): lax.all_to_all(outgoing, 'expert', split_axis=0, concat_axis=0, tiled=True)  384 us
    all_to_all x1, waiting for transfers between devices, local(): lax.all_to_all(returned, 'expert', split_axis=0, concat_axis=0, tiled=True)  361 us
  transfers between devices with their start and end apart: 2, of which 2 were waited for; matrix products, arithmetic and copies ran while one was open for 0% of the time, Pallas kernels for 0%

commit v1 on v0

v1 whole, which is shorter than its diff:
```python
import jax
import jax.numpy as jnp
from jax import lax
from jax.experimental import pallas as pl
from jax.experimental.pallas import tpu as pltpu
from jax.sharding import PartitionSpec as P

MESH = pl.DeviceIdType.MESH
EXPS = 8
CAP = 12
NX = 4
NZ = 16
ROWS = 64
D = 4096
DX = D // NX
UNIT = NX * CAP
PLANE = NX * ROWS
HID = 128
WAVES = ((7, 3), (6, 2), (5, 1), (4, 0))
SEND_ORDER = (7, 3, 6, 2, 5, 1, 4)
PLACE = {t: (w, j) for w, pair in enumerate(WAVES) for j, t in enumerate(pair)}
F32 = jnp.float32
BF16 = jnp.bfloat16


def kernel(
    tok, ids, weights, gain, wg, wu, wd, out,
    normed, rows_in, zsend, xin, wcat, wdn, rs_send, rs_recv, hid,
    own_part, pr_send, pr_recv, ret_send, ret_recv, eo_send, eo_recv, hprev, select, column,
    loc_sem, nx_s, nx_r, wx_s, wx_r, h_s, h_r, z_s, z_r, f_s, f_r, rs_s, rs_r, hd_s, hd_r,
    pr_s, pr_r, rt_s, rt_r, eo_s, eo_r,
):
    sections = lax.axis_size("section")
    sec = lax.axis_index("section")
    me = lax.axis_index("expert")
    z = me // NX
    x = me % NX
    sign = 1 - 2 * (z % 2)
    sec_next = (sec + 1) % sections
    sec_last = (sec + sections - 1) % sections

    def at_z(offset):
        return (sec, ((z + offset + NZ) % NZ) * NX + x)

    def at_x(k):
        return (sec, z * NX + (x + k) % NX)

    def dest_offset(t):
        return 2 * sign * t if t < 4 else -sign * (2 * t - 7)

    def source_offset(t):
        return -2 * sign * t if t < 4 else -sign * (2 * t - 7)

    partner = at_z(sign)

    def remote(src, dst, ssem, rsem, device):
        return pltpu.make_async_remote_copy(
            src_ref=src, dst_ref=dst, send_sem=ssem, recv_sem=rsem,
            device_id=device, device_id_type=MESH,
        )

    pending = []

    def send(*args):
        copy = remote(*args)
        copy.start()
        pending.append(copy)

    barrier = pltpu.get_barrier_semaphore()
    others = [at_x(k) for k in (1, 2, 3)]
    others += [at_z(dest_offset(t)) for t in range(1, 8)]
    others += [at_z(source_offset(t)) for t in range(1, 4)]
    others += [partner]
    others += [(sec_next, z * NX + k) for k in range(NX)]
    others += [(sec_last, z * NX + k) for k in range(NX)]
    for other in others:
        pl.semaphore_signal(barrier, inc=1, device_id=other, device_id_type=MESH)

    own_rows = pl.ds(pl.multiple_of(x * DX, DX), DX)
    own_gate = pl.ds(pl.multiple_of(x * 2 * HID, HID), HID)
    own_up = pl.ds(pl.multiple_of(x * 2 * HID + HID, HID), HID)
    own_hid = pl.ds(pl.multiple_of(x * HID, HID), HID)
    local = [
        pltpu.make_async_copy(wg.at[own_rows, :], wcat.at[:, own_gate], loc_sem.at[0]),
        pltpu.make_async_copy(wu.at[own_rows, :], wcat.at[:, own_up], loc_sem.at[1]),
        pltpu.make_async_copy(wd.at[:, own_rows], wdn.at[own_hid, :], loc_sem.at[2]),
    ]
    for copy in local:
        copy.start()

    total = jnp.zeros((ROWS, 1), F32)
    for c in range(NX):
        part = tok[:, c * DX:(c + 1) * DX].astype(F32)
        total = total + jnp.sum(part * part, axis=1, keepdims=True)
    scale = lax.rsqrt(total / D + 1e-6)
    for c in range(NX):
        part = tok[:, c * DX:(c + 1) * DX].astype(F32)
        part = part * scale * gain[:, c * DX:(c + 1) * DX].astype(F32)
        normed[:, c * DX:(c + 1) * DX] = part.astype(BF16)

    def plane_row(ref):
        return jnp.concatenate([ref[pl.ds(2 * z, 1), :], ref[pl.ds(2 * z + 1, 1), :]], axis=1)

    ids_row = plane_row(ids)
    named = lax.broadcasted_iota(jnp.int32, (16, PLANE), 0) == ids_row
    named = jnp.where(named, 1.0, 0.0)
    early = lax.broadcasted_iota(jnp.int32, (PLANE, PLANE), 0)
    late = lax.broadcasted_iota(jnp.int32, (PLANE, PLANE), 1)
    before = jnp.where((early < late) & (early // ROWS == late // ROWS), 1.0, 0.0).astype(BF16)
    count = jnp.dot(named.astype(BF16), before, preferred_element_type=F32)
    slot = jnp.sum(named * count, axis=0, keepdims=True)
    block = lax.broadcasted_iota(jnp.int32, (1, PLANE), 1) // ROWS
    place = (ids_row * UNIT + block * CAP).astype(F32) + slot
    experts = [((z + dest_offset(t) + NZ) % NZ) // 2 for t in range(EXPS)]

    pl.semaphore_wait(barrier, len(others))

    rows_in[pl.ds(pl.multiple_of(x * ROWS, ROWS), ROWS), :] = normed[:, own_rows]
    own_block = pl.ds(pl.multiple_of(x * ROWS, ROWS), ROWS)
    for k in (1, 3, 2):
        other_cols = pl.ds(pl.multiple_of(((x + k) % NX) * DX, DX), DX)
        send(normed.at[:, other_cols], rows_in.at[own_block, :], nx_s.at[k - 1], nx_r.at[k - 1], at_x(k))
    for k in (1, 3, 2):
        other_rows = pl.ds(pl.multiple_of(((x + k) % NX) * DX, DX), DX)
        send(wg.at[other_rows, :], wcat.at[:, own_gate], wx_s.at[0, k - 1], wx_r.at[0, k - 1], at_x(k))
        send(wu.at[other_rows, :], wcat.at[:, own_up], wx_s.at[1, k - 1], wx_r.at[1, k - 1], at_x(k))
    send(tok, hprev, h_s, h_r, (sec_next, me))

    spread = []
    for t in range(EXPS):
        index = lax.broadcasted_iota(jnp.int32, (UNIT, PLANE), 0) + experts[t] * UNIT
        spread.append(jnp.where(index.astype(F32) == place, 1.0, 0.0).astype(BF16))
    spread = jnp.concatenate(spread, axis=0)

    for k in (1, 3, 2):
        from_block = pl.ds(pl.multiple_of(((x + NX - k) % NX) * ROWS, ROWS), ROWS)
        remote(normed.at[:, own_rows], rows_in.at[from_block, :], nx_s.at[k - 1], nx_r.at[k - 1], at_x(k)).wait_recv()

    for c in range(4):
        cols = slice(c * 256, (c + 1) * 256)
        slotted = jnp.dot(spread, rows_in[:, cols], preferred_element_type=F32).astype(BF16)
        zsend[:, :, cols] = slotted.reshape(EXPS, UNIT, 256)
        w, j = PLACE[0]
        xin[w, j, :, cols] = slotted[:UNIT]

    def forward(t, src):
        w, j = PLACE[t]
        send(src, xin.at[w, 2 + j], f_s.at[t], f_r.at[t], partner)

    for t in SEND_ORDER:
        w, j = PLACE[t]
        send(zsend.at[t], xin.at[w, j], z_s.at[t], z_r.at[t], at_z(dest_offset(t)))
    forward(0, zsend.at[0])
    for k in (1, 3, 2):
        other_cols = pl.ds(pl.multiple_of(((x + k) % NX) * DX, DX), DX)
        send(wd.at[:, other_cols], wdn.at[own_hid, :], wx_s.at[2, k - 1], wx_r.at[2, k - 1], at_x(k))

    eye = early == late
    place_col = jnp.sum(jnp.where(eye, place, 0.0), axis=1, keepdims=True)
    column[...] = jnp.broadcast_to(
        jnp.sum(jnp.where(eye, plane_row(weights), 0.0), axis=1, keepdims=True), column.shape
    )
    key = lax.broadcasted_iota(jnp.int32, (PLANE, EXPS * UNIT), 1)
    shift = jnp.zeros_like(key)
    for t in range(EXPS):
        shift = jnp.where(key // UNIT == t, (experts[t] - t) * UNIT, shift)
    select[...] = jnp.where((key + shift).astype(F32) == place_col, 1.0, 0.0).astype(BF16)

    def wait_landed(wave):
        for t in WAVES[wave]:
            if t:
                w, j = PLACE[t]
                remote(zsend.at[t], xin.at[w, j], z_s.at[t], z_r.at[t], at_z(dest_offset(t))).wait_recv()
                forward(t, xin.at[w, j])

    def gate_up(wave):
        for t in WAVES[wave]:
            w, j = PLACE[t]
            remote(xin.at[w, j], xin.at[w, 2 + j], f_s.at[t], f_r.at[t], partner).wait_recv()
        if wave == 0:
            local[0].wait()
            local[1].wait()
            for k in (1, 3, 2):
                from_x = (x + NX - k) % NX
                cols_g = pl.ds(pl.multiple_of(from_x * 2 * HID, HID), HID)
                cols_u = pl.ds(pl.multiple_of(from_x * 2 * HID + HID, HID), HID)
                remote(wg.at[own_rows, :], wcat.at[:, cols_g], wx_s.at[0, k - 1], wx_r.at[0, k - 1], at_x(k)).wait_recv()
                remote(wu.at[own_rows, :], wcat.at[:, cols_u], wx_s.at[1, k - 1], wx_r.at[1, k - 1], at_x(k)).wait_recv()
        flat = xin[wave].reshape(4 * UNIT, DX)
        for c in range(4):
            cols = slice(c * 256, (c + 1) * 256)
            part = jnp.dot(flat, wcat[:, cols], preferred_element_type=F32).astype(BF16)
            rs_send[wave, :, :, cols] = part.reshape(4, UNIT, 256)
        for k in (1, 3, 2):
            send(rs_send.at[wave, (x + k) % NX], rs_recv.at[wave, k - 1], rs_s.at[wave, k - 1], rs_r.at[wave, k - 1], at_x(k))

    def activate(wave):
        for k in (1, 3, 2):
            remote(rs_send.at[wave, x], rs_recv.at[wave, k - 1], rs_s.at[wave, k - 1], rs_r.at[wave, k - 1], at_x(k)).wait_recv()
        for c in range(NX):
            cols = slice(c * 2 * HID, (c + 1) * 2 * HID)
            both = rs_send[wave, x, :, cols].astype(F32)
            for k in range(3):
                both = both + rs_recv[wave, k, :, cols].astype(F32)
            gate, up = both[:, :HID], both[:, HID:]
            hid[wave, x, :, c * HID:(c + 1) * HID] = (gate / (1.0 + jnp.exp(-gate)) * up).astype(BF16)
        for k in (1, 3, 2):
            send(hid.at[wave, x], hid.at[wave, x], hd_s.at[wave, k - 1], hd_r.at[wave, k - 1], at_x(k))

    def down(wave):
        for k in (1, 3, 2):
            remote(hid.at[wave, x], hid.at[wave, (x + NX - k) % NX], hd_s.at[wave, k - 1], hd_r.at[wave, k - 1], at_x(k)).wait_recv()
        if wave == 0:
            local[2].wait()
            for k in (1, 3, 2):
                from_hid = pl.ds(pl.multiple_of(((x + NX - k) % NX) * HID, HID), HID)
                remote(wd.at[:, own_rows], wdn.at[from_hid, :], wx_s.at[2, k - 1], wx_r.at[2, k - 1], at_x(k)).wait_recv()
        flat = hid[wave].reshape(4 * UNIT, NX * HID)
        for c in range(4):
            cols = slice(c * 256, (c + 1) * 256)
            part = jnp.dot(flat, wdn[:, cols], preferred_element_type=F32)
            for j, t in enumerate(WAVES[wave]):
                own_part[t, :, cols] = part[j * UNIT:(j + 1) * UNIT]
                pr_send[t, :, cols] = part[(2 + j) * UNIT:(3 + j) * UNIT].astype(BF16)
        for t in WAVES[wave]:
            send(pr_send.at[t], pr_recv.at[t], pr_s.at[t], pr_r.at[t], partner)

    def give_back(wave):
        for t in WAVES[wave]:
            remote(pr_send.at[t], pr_recv.at[t], pr_s.at[t], pr_r.at[t], partner).wait_recv()
            both = (own_part[t] + pr_recv[t].astype(F32)).astype(BF16)
            if t:
                ret_send[t] = both
                send(ret_send.at[t], ret_recv.at[t], rt_s.at[t], rt_r.at[t], at_z(source_offset(t)))
            else:
                ret_recv[t] = both

    wait_landed(0)
    gate_up(0)
    wait_landed(1)
    activate(0)
    gate_up(1)
    down(0)
    activate(1)
    give_back(0)
    wait_landed(2)
    down(1)
    gate_up(2)
    give_back(1)
    activate(2)
    wait_landed(3)
    down(2)
    gate_up(3)
    give_back(2)
    activate(3)
    down(3)
    give_back(3)

    for t in range(1, EXPS):
        remote(ret_send.at[t], ret_recv.at[t], rt_s.at[t], rt_r.at[t], at_z(source_offset(t))).wait_recv()
    for c in range(4):
        cols = slice(c * 256, (c + 1) * 256)
        back = ret_recv[:, :, cols].reshape(EXPS * UNIT, 256)
        rows = jnp.dot(select[...], back, preferred_element_type=F32)
        rows = rows * jnp.concatenate([column[...], column[...]], axis=1)
        eo_send[:, :, cols] = rows.astype(BF16).reshape(NX, ROWS, 256)
    for k in range(NX):
        xo = (x + k) % NX
        send(eo_send.at[xo], eo_recv.at[x], eo_s.at[k], eo_r.at[k], (sec_next, z * NX + xo))

    remote(tok, hprev, h_s, h_r, (sec_next, me)).wait_recv()
    for k in range(NX):
        xf = (x + NX - k) % NX
        remote(eo_send.at[x], eo_recv.at[xf], eo_s.at[k], eo_r.at[k], (sec_next, me)).wait_recv()
    for c in range(NX):
        cols = slice(c * DX, (c + 1) * DX)
        out[:, cols] = (hprev[:, cols].astype(F32) + eo_recv[c].astype(F32)).astype(BF16)
    for copy in pending:
        copy.wait_send()


def local(tokens, expert_ids, gate_weights, norm_gain, w_gate, w_up, w_down):
    vmem = pl.BlockSpec(memory_space=pltpu.VMEM)
    hbm = pl.BlockSpec(memory_space=pl.ANY)
    dma = pltpu.SemaphoreType.DMA
    scratch = [
        pltpu.VMEM((ROWS, D), BF16),
        pltpu.VMEM((PLANE, DX), BF16),
        pltpu.VMEM((EXPS, UNIT, DX), BF16),
        pltpu.VMEM((4, 4, UNIT, DX), BF16),
        pltpu.VMEM((DX, 2 * NX * HID), BF16),
        pltpu.VMEM((NX * HID, DX), BF16),
        pltpu.VMEM((4, NX, UNIT, 2 * NX * HID), BF16),
        pltpu.VMEM((4, 3, UNIT, 2 * NX * HID), BF16),
        pltpu.VMEM((4, NX, UNIT, NX * HID), BF16),
        pltpu.VMEM((EXPS, UNIT, DX), F32),
        pltpu.VMEM((EXPS, UNIT, DX), BF16),
        pltpu.VMEM((EXPS, UNIT, DX), BF16),
        pltpu.VMEM((EXPS, UNIT, DX), BF16),
        pltpu.VMEM((EXPS, UNIT, DX), BF16),
        pltpu.VMEM((NX, ROWS, DX), BF16),
        pltpu.VMEM((NX, ROWS, DX), BF16),
        pltpu.VMEM((ROWS, D), BF16),
        pltpu.VMEM((PLANE, EXPS * UNIT), BF16),
        pltpu.VMEM((PLANE, 128), F32),
        dma((3,)), dma((3,)), dma((3,)), dma((3, 3)), dma((3, 3)), dma(()), dma(()),
        dma((8,)), dma((8,)), dma((8,)), dma((8,)), dma((4, 3)), dma((4, 3)), dma((4, 3)), dma((4, 3)),
        dma((8,)), dma((8,)), dma((8,)), dma((8,)), dma((4,)), dma((4,)),
    ]
    result = pl.pallas_call(
        kernel,
        out_shape=jax.ShapeDtypeStruct((ROWS, D), BF16),
        in_specs=[vmem, vmem, vmem, vmem, hbm, hbm, hbm],
        out_specs=vmem,
        scratch_shapes=scratch,
        name="moe_stop",
        compiler_params=pltpu.CompilerParams(
            collective_id=0, has_side_effects=True, vmem_limit_bytes=48 * 1024 * 1024
        ),
    )(
        tokens[0],
        expert_ids.reshape(32, 128),
        gate_weights.reshape(32, 128),
        norm_gain,
        w_gate[0],
        w_up[0],
        w_down[0],
    )
    return result[None]


def solution(mesh):
    placed = (
        P("section", "expert", None),
        P("section", None, None, None),
        P("section", None, None, None),
        P("section", None),
        P("section", None, "expert"),
        P("section", None, "expert"),
        P("section", "expert", None),
    )
    return jax.shard_map(
        local, mesh=mesh, in_specs=placed, out_specs=P("section", "expert", None), check_vma=False
    )
```

time: 824 us -> 154 us (0.19)
  blocking collectives: 384 us -> 0 us
  waiting for transfers between devices: 367 us -> 0 us
  Pallas kernels: 0 us -> 146 us
  starting transfers between devices: 21.3 us -> 0 us
  matrix products: 19.5 us -> 0 us
  local copies, waits for them, and re-layouts: 23.4 us -> 7.66 us
    all_to_all x1 -> x0, blocking collectives: 384 us -> none  [local(): lax.all_to_all(outgoing, 'expert', split_axis=0, concat_axis=0, tiled=True)]
    all_to_all x1 -> x0, waiting for transfers between devices: 361 us -> none  [local(): lax.all_to_all(returned, 'expert', split_axis=0, concat_axis=0, tiled=True)]
    pallas_call x0 -> x1, Pallas kernels: none -> 146 us  [local(): pl.pallas_call(kernel, out_shape=jax.ShapeDtypeStruct((ROWS, D), BF16), i...]
    reshape x2 -> x0, local copies, waits for them, and re-layouts: 19.8 us -> none  [the longest x1 10.1 us: local(): flat_rows = slotted.reshape(-1, width)]
    dot_general x4 -> x0, matrix products: 19.5 us -> none  [the longest x1 12.1 us: local(): jnp.dot(hidden, down_rows, preferred_element_type=jnp.float32)]
    all_to_all x1 -> x0, starting transfers between devices: 11.1 us -> none  [local(): lax.all_to_all(returned, 'expert', split_axis=0, concat_axis=0, tiled=True)]
    ppermute x1 -> x0, starting transfers between devices: 10.2 us -> none  [from_behind(): return lax.ppermute(value, axis, pairs)]
  transfers between devices with their start and end apart: 2 -> 0, of which waited for: 2 -> 0; matrix products, arithmetic and copies ran while one was open for 0% -> 0% of each run, Pallas kernels for 0% -> 0%
where the time goes in v1:
time: 154 us; the launch traced here: 153 us
  Pallas kernels  146 us (95%)
  local copies, waits for them, and re-layouts  7.66 us (5%)
    pallas_call x1, Pallas kernels, local(): pl.pallas_call(kernel, out_shape=jax.ShapeDtypeStruct((ROWS, D), BF16), i...  146 us
    unnamed x15, local copies, waits for them, and re-layouts  7.66 us

profile of v1, /device:TPU:1, one launch (start us, length us, event | category | flops | bytes accessed | tf_op | source)
XLA Modules:
  0.0 153.3 jit_solution(8508510560231577929)
XLA Ops:
  0.0 0.0 copy-start
  0.0 1.2 copy-done
  1.2 0.0 copy-start.1
  1.2 1.2 copy-done.1
  2.5 0.0 copy-start.2
  2.5 1.2 copy-done.2
  3.7 0.0 copy-start.3
  3.7 1.0 copy-done.3
  4.7 0.0 copy-start.4
  4.7 0.7 copy-done.4
  5.4 0.0 copy-start.5
  5.4 0.7 copy-done.5
  6.2 0.0 copy-start.6
  6.2 0.7 copy-done.6
  6.9 145.6 %moe_stop.1 = bf16[64,4096]{1,0:T(8,128)(2,1)S(1)} custom-call(bf16[64,4096]{1,0:T(8,128)(2,1)S(1)} %bitcast.11, s32[32,128]{1,0:T(8,128)S(1)} %bitcast.12, f32[32,128]{1,0:T(8,128)S(1)} %bitcast.13, bf16[1,4096]{1,0:T(2,128)(2,1)S(1)} %copy-done.6, bf16[4096,128]{1,0:T(8,128)(2,1)S(1)} %bitcast.8, bf16[4096,128]{1,0:T(8,128)(2,1)S(1)} %bitcast.9, ...), custom_call_target="tpu_custom_call" | custom-call | tf_op jit(solution)/shard_map/moe_stop/pallas_call | solution.py:310
  152.5 0.8 copy.9
Async XLA Ops:
  0.0 1.2 copy-start
  1.2 1.2 copy-start.1
  2.5 1.2 copy-start.2
  3.7 1.0 copy-start.3
  4.7 0.7 copy-start.4
  5.4 0.7 copy-start.5
  6.2 0.7 copy-start.6
